TPU v7x, 32 devices: a whole 2x2x4 slice. The times are simulated.
32 devices in a mesh: context: 4 (over z), dp: 4 (over y, core), head: 2 (over x).
Axes of the slice: x: 2, y: 2, z: 4, core: 2. Of those that a mesh axis runs over, the one named last changes fastest.
Arguments:
- inputs: bfloat16 [4, 512, 2304], P('dp', 'context', 'head'), may hold values from -6 to 6
- output_grad: bfloat16 [4, 512, 2304], P('dp', 'context', 'head'), may hold values from -6 to 6
- qkv_weight: bfloat16 [2304, 3, 4096], P(None, None, 'head'), may hold values from -0.125 to 0.125
- out_weight: bfloat16 [2304, 4096], P(None, 'head'), may hold values from -0.09375 to 0.09375
- down_weight: bfloat16 [2304, 128], replicated, may hold values from -0.125 to 0.125
- up_weight: bfloat16 [128, 4096], P(None, 'head'), may hold values from -0.5 to 0.5
- beta_weight: bfloat16 [2304, 32], P(None, 'head'), may hold values from -0.125 to 0.125
- gate_bias: float32 [4096], P('head'), may hold values from -9 to -1.6, as said below
Outputs:
- layer_out: bfloat16 [4, 512, 2304], P('dp', 'context', 'head')
- input_grad: bfloat16 [4, 512, 2304], P('dp', 'context', 'head')
- qkv_grad: bfloat16 [2304, 3, 4096], P(('context', 'dp'), None, 'head')
- out_grad: bfloat16 [2304, 4096], P(('context', 'dp'), 'head')
- up_grad: float32 [128, 4096], P(None, 'head')
- down_grad: float32 [2304, 128], replicated
- beta_grad: float32 [2304, 32], P(None, 'head')
- bias_grad: float32 [4096], P('head')
Inputs may be any that keep to these rules, and one draw needn't show every extreme that they name: `gate_bias`: offsets of the decay gate, one per channel.
All inputs are finite; a program needn't handle non-finite values.
Results may differ from a plain program's by a relative error of at most 0.02.
Values may be sent and summed in bfloat16 or wider, within the bound.
A program may use at most 192 MiB of HBM per device.

v0:
```python
import jax
import jax.numpy as jnp
from jax import lax
from jax.sharding import PartitionSpec as P

SPAN = 64
epsilon = 1e-06
highest = lax.Precision.HIGH


def shifted(value, axis, by):
    count = lax.axis_size(axis)
    pairs = [(i, i + by) for i in range(count) if 0 <= i + by < count]
    return lax.ppermute(value, axis, pairs)


def product(pattern, left, right):
    return jnp.einsum(pattern, left, right, precision=highest)


def activate(projected, gate_pre, beta_logit):
    token_count = projected.shape[0]
    head_count = beta_logit.shape[1]
    head_width = projected.shape[2] // head_count
    blocks = projected.reshape(token_count, 3, head_count, head_width)

    def normalize(values):
        return values * lax.rsqrt(jnp.sum(values * values, axis=-1, keepdims=True) + epsilon)

    queries = jnp.swapaxes(normalize(blocks[:, 0]), 0, 1)
    key_rows = jnp.swapaxes(normalize(blocks[:, 1]), 0, 1)
    value_rows = jnp.swapaxes(blocks[:, 2], 0, 1)
    decays = jnp.swapaxes(
        (-0.25 * jax.nn.sigmoid(gate_pre)).reshape(token_count, head_count, head_width), 0, 1
    )
    betas = jnp.swapaxes(jax.nn.sigmoid(beta_logit), 0, 1)
    return (queries, key_rows, value_rows, decays, betas)


def span_terms(queries, key_rows, value_rows, decays, betas):
    leading = queries.shape[:-2]
    block_count = queries.shape[-2] // SPAN

    def blocked(member):
        return member.reshape(leading + (block_count, SPAN) + member.shape[-1:])

    queries, key_rows, value_rows, decays = (
        blocked(queries),
        blocked(key_rows),
        blocked(value_rows),
        blocked(decays),
    )
    betas = betas.reshape(leading + (block_count, SPAN))
    cumulative = jnp.cumsum(decays, axis=-2)
    middle = cumulative[..., SPAN // 2 - 1 : SPAN // 2, :]
    final_decay = cumulative[..., SPAN - 1 :, :]
    key_fwd = jnp.exp(cumulative - middle) * key_rows
    key_back = jnp.exp(middle - cumulative) * key_rows
    query_fwd = jnp.exp(cumulative - middle) * queries
    key_start = jnp.exp(cumulative) * key_rows
    query_start = jnp.exp(cumulative) * queries
    key_end = jnp.exp(final_decay - cumulative) * key_rows
    row_index = lax.broadcasted_iota(jnp.int32, (SPAN, SPAN), 0)
    col_index = lax.broadcasted_iota(jnp.int32, (SPAN, SPAN), 1)
    strict = (row_index > col_index).astype(jnp.float32)
    lower_mask = (row_index >= col_index).astype(jnp.float32)
    coupling = betas[..., :, None] * product("...tc,...sc->...ts", key_fwd, key_back) * strict
    powers = -coupling
    inverse = jnp.eye(SPAN, dtype=jnp.float32) + powers
    for section in range(1, (SPAN - 1).bit_length()):
        powers = product("...ts,...su->...tu", powers, powers)
        inverse = inverse + product("...ts,...su->...tu", inverse, powers)
    solver = inverse * betas[..., None, :]
    solved_values = product("...ts,...sc->...tc", solver, value_rows)
    solved_keys = product("...ts,...sc->...tc", solver, key_start)
    scores = product("...tc,...sc->...ts", query_fwd, key_back) * lower_mask
    query_eff = query_start - product("...ts,...sc->...tc", scores, solved_keys)
    local_out = product("...ts,...sc->...tc", scores, solved_values)
    side = queries.shape[-1]
    diagonal = jnp.eye(side, dtype=jnp.float32) * jnp.exp(final_decay)[..., 0, :, None]
    transition = diagonal - product("...sc,...sd->...cd", key_end, solved_keys)
    offset = product("...sc,...sd->...cd", key_end, solved_values)
    return (query_eff, local_out, transition, offset)


def chain(terms, state_in):

    def chain_advance(carried, pieces):
        query_eff, local_out, transition, offset = pieces
        emitted = product("...tc,...cd->...td", query_eff, carried) + local_out
        return (product("...cd,...de->...ce", transition, carried) + offset, emitted)

    moved = tuple((jnp.moveaxis(member, -3, 0) for member in terms))
    final_state, emitted = lax.scan(chain_advance, state_in, moved)
    return (jnp.moveaxis(emitted, 0, -3), final_state)


def compose_spans(transition, offset, identity):

    def compose_advance(carried, pieces):
        return (
            (
                product("hcd,hde->hce", pieces[0], carried[0]),
                product("hcd,hde->hce", pieces[0], carried[1]) + pieces[1],
            ),
            None,
        )

    moved = (jnp.moveaxis(transition, -3, 0), jnp.moveaxis(offset, -3, 0))
    combined, unused_rows = lax.scan(compose_advance, (identity, jnp.zeros_like(identity)), moved)
    return combined


def shards(
    inputs, output_grad, qkv_weight, out_weight, down_weight, up_weight, beta_weight, gate_bias
):
    gathered = lax.all_gather(inputs, "head", axis=2, tiled=True)[0]
    token_count, model_width = gathered.shape
    all_width = qkv_weight.shape[2]
    head_count = beta_weight.shape[1]
    head_width = all_width // head_count
    qkv_flat = qkv_weight.reshape(model_width, 3 * all_width)
    projected = jnp.dot(gathered, qkv_flat, preferred_element_type=jnp.float32).reshape(
        token_count, 3, all_width
    )
    low_rank = jnp.dot(gathered, down_weight, preferred_element_type=jnp.float32).astype(
        jnp.bfloat16
    )
    gate_pre = jnp.dot(low_rank, up_weight, preferred_element_type=jnp.float32) + gate_bias
    beta_logit = jnp.dot(gathered, beta_weight, preferred_element_type=jnp.float32)
    acts, act_vjp = jax.vjp(activate, projected, gate_pre, beta_logit)
    terms, terms_vjp = jax.vjp(span_terms, *acts)
    identity = jnp.broadcast_to(
        jnp.eye(head_width, dtype=jnp.float32), (head_count, head_width, head_width)
    )
    empty = jnp.zeros((head_count, head_width, head_width), jnp.float32)
    shard_linear, shard_offset = compose_spans(terms[2], terms[3], identity)
    grad_whole = lax.all_gather(output_grad, "head", axis=2, tiled=True)[0]
    mixed_grad = jnp.dot(grad_whole, out_weight, preferred_element_type=jnp.float32)
    grad_blocks = jnp.swapaxes(
        mixed_grad.reshape(token_count, head_count, head_width), 0, 1
    ).reshape(terms[1].shape)
    own_grad = jnp.zeros_like(empty)
    for block in reversed(range(token_count // SPAN)):
        own_grad = product("hcd,hce->hde", terms[2][:, block], own_grad) + product(
            "htc,htd->hcd", terms[0][:, block], grad_blocks[:, block]
        )
    linear_back = jnp.swapaxes(shard_linear, 1, 2)
    shard_count = lax.axis_size("context")
    shard_index = lax.axis_index("context")
    state_in, state_grad = (empty, empty)
    for step in range(shard_count - 1):
        leaving = shard_offset
        leaving_grad = own_grad
        if step:
            leaving = product("hcd,hde->hce", shard_linear, state_in) + leaving
            leaving_grad = product("hcd,hde->hce", linear_back, state_grad) + leaving_grad
        state_in = shifted(leaving.astype(jnp.bfloat16), "context", 1).astype(jnp.float32)
        state_grad = shifted(leaving_grad.astype(jnp.bfloat16), "context", -1).astype(jnp.float32)
    (mixed_blocks, final_state), chain_vjp = jax.vjp(chain, terms, state_in)
    mixed = jnp.swapaxes(mixed_blocks.reshape(head_count, token_count, head_width), 0, 1)
    mixed = mixed.reshape(token_count, all_width).astype(jnp.bfloat16)
    slab = model_width // shard_count

    def slab_of(member):
        whole = lax.all_gather(member, "context", axis=0, tiled=True)
        return lax.dynamic_slice_in_dim(whole, shard_index * slab, slab, axis=1)

    def weight_term(rows, columns):
        whole = lax.all_gather(columns, "context", axis=0, tiled=True)
        term = jnp.einsum("tr,tc->rc", rows, whole, preferred_element_type=jnp.float32)
        return lax.psum_scatter(term.astype(jnp.bfloat16), "dp", scatter_dimension=0, tiled=True)

    input_slab = slab_of(gathered)
    grad_slab = slab_of(grad_whole)
    out_grad = weight_term(grad_slab, mixed)
    out_part = jnp.einsum("tc,dc->td", mixed, out_weight, preferred_element_type=jnp.float32)
    layer_out = lax.psum_scatter(
        out_part.astype(jnp.bfloat16), "head", scatter_dimension=1, tiled=True
    )[None]
    term_grads, unused_state = chain_vjp((grad_blocks, state_grad))
    proj_grad, pre_grad, logit_grad = act_vjp(terms_vjp(term_grads))
    proj_parts = [proj_grad[:, part].astype(jnp.bfloat16) for part in range(3)]
    qkv_grad = jnp.stack([weight_term(input_slab, part) for part in proj_parts], axis=1)
    gate_low = pre_grad.astype(jnp.bfloat16)
    logit_low = logit_grad.astype(jnp.bfloat16)
    low_grad = jnp.einsum(
        "tc,rc->tr", gate_low, up_weight, preferred_element_type=jnp.float32
    ).astype(jnp.bfloat16)
    up_term = jnp.einsum("tr,tc->rc", low_rank, gate_low, preferred_element_type=jnp.float32)
    beta_term = jnp.einsum("td,th->dh", gathered, logit_low, preferred_element_type=jnp.float32)
    bias_term = jnp.sum(pre_grad, axis=0)
    down_term = jnp.einsum("td,tr->dr", gathered, low_grad, preferred_element_type=jnp.float32)
    small = [up_term, down_term, beta_term, bias_term]
    packed = jnp.concatenate([term.astype(jnp.bfloat16).reshape(-1, 128) for term in small], axis=0)
    packed = lax.psum(packed, ("context", "dp")).astype(jnp.float32)
    results, start = ([], 0)
    for term in small:
        count = term.size // 128
        results.append(packed[start : start + count].reshape(term.shape))
        start += count
    up_grad, down_grad, beta_grad, bias_grad = results
    down_grad = lax.psum(down_grad, "head")
    input_part = jnp.einsum("tr,dr->td", low_grad, down_weight, preferred_element_type=jnp.float32)
    input_part = input_part + jnp.einsum(
        "th,dh->td", logit_low, beta_weight, preferred_element_type=jnp.float32
    )
    input_part = input_part + jnp.einsum(
        "tc,dc->td",
        jnp.concatenate(proj_parts, axis=1),
        qkv_flat,
        preferred_element_type=jnp.float32,
    )
    input_grad = lax.psum_scatter(
        input_part.astype(jnp.bfloat16), "head", scatter_dimension=1, tiled=True
    )[None]
    return (layer_out, input_grad, qkv_grad, out_grad, up_grad, down_grad, beta_grad, bias_grad)


def solution(mesh):
    return jax.shard_map(
        shards,
        mesh=mesh,
        in_specs=(
            P("dp", "context", "head"),
            P("dp", "context", "head"),
            P(None, None, "head"),
            P(None, "head"),
            P(),
            P(None, "head"),
            P(None, "head"),
            P("head"),
        ),
        out_specs=(
            P("dp", "context", "head"),
            P("dp", "context", "head"),
            P(("context", "dp"), None, "head"),
            P(("context", "dp"), "head"),
            P(None, "head"),
            P(),
            P(None, "head"),
            P("head"),
        ),
        check_vma=False,
    )
```

profile of v0, /device:TPU:0, one launch (start us, length us, event | category | flops | bytes accessed | tf_op | source)
XLA Modules:
  0.0 760.1 jit_solution(1291417502378739657)
XLA Ops:
  8.1 11.0 %all_gather.24 = bf16[1,128,2304]{2,1,0:T(8,128)(2,1)S(1)} all-gather(bf16[1,128,1152]{2,1,0:T(8,128)(2,1)} %param.14), channel_id=1, replica_groups=mesh['context'=4,'dp'=4,'head'=2] {'head'}, dimensions={2}, use_global_device_ids=true | all-gather | bytes 884736 | tf_op jit(solution)/shard_map/all_gather | solution.py:117
  22.9 35.1 %copy.152 = bf16[2304,3,2048]{0,2,1:T(8,128)(2,1)} copy(bf16[2304,3,2048]{2,0,1:T(8,128)(2,1)} %param.16) | data formatting | bytes 56623104 | tf_op args[2]
  58.0 15.4 %fusion.134 = f32[128,3,16,128]{3,0,2,1:T(8,128)} fusion(bf16[3,16,128,2304]{3,2,1,0:T(8,128)(2,1)} %bitcast.472, bf16[1,128,2304]{2,1,0:T(8,128)(2,1)S(1)} %all_gather.24), kind=kOutput, calls=%fused_computation.216 | convolution fusion | flops 3623878656 | bytes 32047104 | tf_op jit(solution)/shard_map/dot_general | solution.py:123
  107.0 12.9 %while.51 = (s32[]{:T(128)}, f32[16,128,128]{2,1,0:T(8,128)}, f32[16,128,128]{2,1,0:T(8,128)}, f32[2,16,128,128]{3,2,1,0:T(8,128)}, f32[2,16,128,128]{3,2,1,0:T(8,128)}, /*index=5*/s32[]{:T(128)}, s32[]{:T(128)}) while((s32[]{:T(128)}, f32[16,128,128]{2,1,0:T(8,128)}, f32[16,128,128]{2,1,0:T(8,128)}, ...), condition=%wide.region_3.4_spmd.clone, body=%wide.region_2.0_spmd.clone.sunk | while | flops 403177472 | bytes 24118416 | solution.py:110
  134.9 8.4 %all_gather.25 = bf16[1,128,2304]{2,1,0:T(8,128)(2,1)} all-gather(bf16[1,128,1152]{2,1,0:T(8,128)(2,1)S(1)} %copy-done.97), channel_id=1, replica_groups=mesh['context'=4,'dp'=4,'head'=2] {'head'}, dimensions={2}, use_global_device_ids=true | all-gather | bytes 884736 | tf_op jit(solution)/shard_map/all_gather | solution.py:138
  143.2 13.1 %copy.257 = bf16[2048,2304]{1,0:T(8,128)(2,1)} copy(bf16[2048,2304]{0,1:T(8,128)(2,1)} %bitcast.482) | data formatting | bytes 18874368 | tf_op jit(solution)/shard_map/dot_general | solution.py:139
  156.4 5.8 fusion.136
  172.4 5.4 collective-permute-start.1
  201.7 9.2 %while.49 = (s32[]{:T(128)}, f32[16,128,128]{2,1,0:T(8,128)S(1)}, bf16[2,16,64,128]{3,2,0,1:T(8,128)(2,1)}, f32[2,16,128,128]{3,2,1,0:T(8,128)}, f32[2,16,128,12...) while((s32[]{:T(128)}, f32[16,128,128]{2,1,0:T(8,128)S(1)}, ...), condition=%wide.region_6.7_spmd, body=%wide.region_5.6_spmd.sunk | while | flops 302383104 | bytes 36178636 | solution.py:94
  217.5 23.3 %while.50 = (s32[]{:T(128)}, f32[16,128,128]{2,1,0:T(8,128)S(1)}, f32[2,16,64,128]{3,2,0,1:T(8,128)}, f32[2,16,64,128]{3,2,1,0:T(8,128)}, f32[2,16,128,128]{2,3,...) while((s32[]{:T(128)}, f32[16,128,128]{2,1,0:T(8,128)S(1)}, ...), condition=%wide.region_9.10_spmd, body=%wide.region_8.9_spmd.sunk | while | flops 604241920 | bytes 56627016 | solution.py:94
  290.5 4.5 fusion.66
  332.9 11.5 %fusion.57 = f32[128,2304]{1,0:T(8,128)S(1)} fusion(bf16[2304,6144]{0,1:T(8,128)(2,1)} %bitcast.473, bf16[128,2048]{0,1:T(8,128)(2,1)S(1)} %copy-done.93, bf16[128,2048]{0,1:T(8,128)(2,1)S(1)} %get-tuple-element.464, bf16[128,2048]{0,1:T(8,128)(2,1)S(1)} %get-tuple-element.463), kind=kOutput, calls=%fused_computation.83 | convolution fusion | flops 3628597248 | bytes 31064064 | tf_op jit(solution)/shard_map/tc,dc->td/dot_general | solution.py:208
  346.1 7.1 convolution_convert_fusion.1
  354.3 175.0 %all-reduce.8.cloned.1.call-done = bf16[4656,128]{0,1:T(8,128)(2,1)} async-done(((bf16[4656,128]{0,1:T(8,128)(2,1)}), bf16[4656,128]{0,1:T(8,128)(2,1)}) %all-reduce.8.cloned.1.call-update) | async-done | bytes 1191952 | tf_op jit(solution)/shard_map/psum | solution.py:196
  531.6 5.1 convolution_convert_fusion.6
  538.5 4.9 convolution_convert_fusion.5
  543.5 4.9 convolution_convert_fusion.4
  548.5 21.4 %all-gather.22.cloned.1.call-done = bf16[1,512,2304]{2,1,0:T(8,128)(2,1)} async-done(((bf16[1,128,2304]{2,1,0:T(8,128)(2,1)}), bf16[1,512,2304]{2,1,0:T(8,128)(2,1)}) %all-gather.22.cloned.1.call-update) | async-done | bytes 2359312 | tf_op jit(solution)/shard_map/all_gather | solution.py:166
  569.9 47.1 %all-gather.12.cloned.1.call-done = bf16[512,2048]{0,1:T(8,128)(2,1)} async-done(((bf16[128,2048]{0,1:T(8,128)(2,1)}), bf16[512,2048]{0,1:T(8,128)(2,1)}) %all-gather.12.cloned.1.call-update) | async-done | bytes 2097168 | tf_op jit(solution)/shard_map/all_gather | solution.py:170
  616.9 5.6 convolution_convert_fusion.3
  636.2 9.6 %reduce-scatter.11.cloned.1.call-done = bf16[144,2048]{1,0:T(8,128)(2,1)} async-done(((bf16[576,2048]{1,0:T(8,128)(2,1)}), bf16[144,2048]{1,0:T(8,128)(2,1)}) %reduce-scatter.11.cloned.1.call-update) | async-done | bytes 589840 | tf_op jit(solution)/shard_map/reduce_scatter | solution.py:172
  645.8 35.2 %reduce-scatter.13.cloned.1.call-done = bf16[144,2048]{1,0:T(8,128)(2,1)} async-done(((bf16[576,2048]{1,0:T(8,128)(2,1)}), bf16[144,2048]{1,0:T(8,128)(2,1)}) %reduce-scatter.13.cloned.1.call-update) | async-done | bytes 589840 | tf_op jit(solution)/shard_map/reduce_scatter | solution.py:172
  681.1 35.4 %reduce-scatter.15.cloned.1.call-done = bf16[144,2048]{1,0:T(8,128)(2,1)} async-done(((bf16[576,2048]{1,0:T(8,128)(2,1)}), bf16[144,2048]{1,0:T(8,128)(2,1)}) %reduce-scatter.15.cloned.1.call-update) | async-done | bytes 589840 | tf_op jit(solution)/shard_map/reduce_scatter | solution.py:172
  719.3 33.1 %reduce-scatter.17.cloned.1.call-done = bf16[144,2048]{1,0:T(8,128)(2,1)} async-done(((bf16[576,2048]{1,0:T(8,128)(2,1)}), bf16[144,2048]{1,0:T(8,128)(2,1)}) %reduce-scatter.17.cloned.1.call-update) | async-done | bytes 589840 | tf_op jit(solution)/shard_map/reduce_scatter | solution.py:172
  (452 shorter events, 247.5 us)
Async XLA Ops:
  8.0 521.3 %all-reduce.8.cloned.1.call-start = ((), (), s32[]{:S(2)}) async-start(), calls=%async_computation.11 | async-start | bytes 2424832 | tf_op jit(solution)/shard_map/psum | solution.py:196
  19.1 294.2 %copy-start.37 = (bf16[1,128,2304]{2,1,0:T(8,128)(2,1)}, bf16[1,128,2304]{2,1,0:T(8,128)(2,1)S(1)}, u32[]{:S(2)}) copy-start(bf16[1,128,2304]{2,1,0:T(8,128)(2,1)S(1)} %all_gather.24) | copy-start | bytes 1769476
  81.2 45.5 %copy-start.3 = (f32[128,16,128]{2,0,1:T(8,128)}, f32[128,16,128]{2,0,1:T(8,128)S(1)}, u32[]{:S(2)}) copy-start(f32[128,16,128]{2,0,1:T(8,128)S(1)} %get-tuple-element.459) | copy-start | bytes 3145732
  122.2 47.9 %collective-permute-start = (bf16[16,128,128]{2,1,0:T(8,128)(2,1)}, bf16[16,128,128]{2,1,0:T(8,128)(2,1)}, u32[]{:S(2)}, u32[]{:S(2)}) collective-permute-start(bf16[16,128,128]{2,1,0:T(8,128)(2,1)} %convert_element_type.153), channel_id=1, source_target_pairs={{0,8},{8,16},{16,24},{1,9},{9,17},{17,25},{2,10},{10,18},{18,26},{... | collective-permute-start | bytes 1572872 | tf_op jit(solution)/shard_map/ppermute | solution.py:14
  130.2 32.1 %copy-start.72 = (f32[16,2,64,128]{3,2,1,0:T(8,128)}, f32[16,2,64,128]{3,2,1,0:T(8,128)S(1)}, u32[]{:S(2)}) copy-start(f32[16,2,64,128]{3,2,1,0:T(8,128)S(1)} %convolution_subtract_fusion) | copy-start | bytes 3145732
  168.7 13.9 %collective-permute-start.3 = (bf16[16,128,128]{2,1,0:T(8,128)(2,1)}, bf16[16,128,128]{2,1,0:T(8,128)(2,1)}, u32[]{:S(2)}, u32[]{:S(2)}) collective-permute-start(bf16[16,128,128]{2,1,0:T(8,128)(2,1)} %get-tuple-element.474), channel_id=1, source_target_pairs={{8,0},{16,8},{24,16},{9,1},{17,9},{25,17},{10,2},{18,10},{26,18},{... | collective-permute-start | bytes 1572872 | tf_op jit(solution)/shard_map/ppermute | solution.py:14
  172.4 13.7 %collective-permute-start.1 = (bf16[16,128,128]{2,1,0:T(8,128)(2,1)}, bf16[16,128,128]{2,1,0:T(8,128)(2,1)}, u32[]{:S(2)}, u32[]{:S(2)}) collective-permute-start(bf16[16,128,128]{2,1,0:T(8,128)(2,1)} %fusion.77), channel_id=1, source_target_pairs={{0,8},{8,16},{16,24},{1,9},{9,17},{17,25},{2,10},{10,18},{18,26},{... | collective-permute-start | bytes 1572872 | tf_op jit(solution)/shard_map/ppermute | solution.py:14
  184.4 12.8 %collective-permute-start.4 = (bf16[16,128,128]{2,1,0:T(8,128)(2,1)S(1)}, bf16[16,128,128]{2,1,0:T(8,128)(2,1)S(1)}, u32[]{:S(2)}, u32[]{:S(2)}) collective-permute-start(bf16[16,128,128]{2,1,0:T(8,128)(2,1)S(1)} %fusion.79), channel_id=1, source_target_pairs={{8,0},{16,8},{24,16},{9,1},{17,9},{25,17},{10,2},{18,10},{26,18},{... | collective-permute-start | bytes 1572872 | tf_op jit(solution)/shard_map/ppermute | solution.py:14
  187.7 12.4 %collective-permute-start.2 = (bf16[16,128,128]{2,1,0:T(8,128)(2,1)S(1)}, bf16[16,128,128]{2,1,0:T(8,128)(2,1)S(1)}, u32[]{:S(2)}, u32[]{:S(2)}) collective-permute-start(bf16[16,128,128]{2,1,0:T(8,128)(2,1)S(1)} %fusion.78), channel_id=1, source_target_pairs={{0,8},{8,16},{16,24},{1,9},{9,17},{17,25},{2,10},{10,18},{18,26},{... | collective-permute-start | bytes 1572872 | tf_op jit(solution)/shard_map/ppermute | solution.py:14
  198.8 12.2 %collective-permute-start.5 = (bf16[16,128,128]{2,1,0:T(8,128)(2,1)}, bf16[16,128,128]{2,1,0:T(8,128)(2,1)}, u32[]{:S(2)}, u32[]{:S(2)}) collective-permute-start(bf16[16,128,128]{2,1,0:T(8,128)(2,1)} %fusion.80), channel_id=1, source_target_pairs={{8,0},{16,8},{24,16},{9,1},{17,9},{25,17},{10,2},{18,10},{26,18},{... | collective-permute-start | bytes 1572872 | tf_op jit(solution)/shard_map/ppermute | solution.py:14
  258.3 12.3 %copy-start.74 = (f32[16,2,64,64]{3,2,1,0:T(8,128)}, f32[16,2,64,64]{3,2,1,0:T(8,128)S(1)}, u32[]{:S(2)}) copy-start(f32[16,2,64,64]{3,2,1,0:T(8,128)S(1)} %convolution_add_fusion.7) | copy-start | bytes 1572868
  318.0 213.6 %all-gather.14.cloned.1.call-start = ((), (), s32[]{:S(2)}) async-start(), calls=%async_computation.13 | async-start | bytes 2949120 | tf_op jit(solution)/shard_map/all_gather | solution.py:166
  318.6 213.0 %all-gather.16.cloned.1.call-start = ((), (), s32[]{:S(2)}) async-start(), calls=%async_computation.14 | async-start | bytes 2621440 | tf_op jit(solution)/shard_map/all_gather | solution.py:170
  329.3 207.6 %all-gather.18.cloned.1.call-start = ((), (), s32[]{:S(2)}) async-start(), calls=%async_computation.15 | async-start | bytes 2621440 | tf_op jit(solution)/shard_map/all_gather | solution.py:170
  329.9 213.6 %all-gather.20.cloned.1.call-start = ((), (), s32[]{:S(2)}) async-start(), calls=%async_computation.16 | async-start | bytes 2621440 | tf_op jit(solution)/shard_map/all_gather | solution.py:170
  330.6 239.2 %all-gather.22.cloned.1.call-start = ((), (), s32[]{:S(2)}) async-start(), calls=%async_computation.17 | async-start | bytes 2949120 | tf_op jit(solution)/shard_map/all_gather | solution.py:166
  331.4 285.6 %all-gather.12.cloned.1.call-start = ((), (), s32[]{:S(2)}) async-start(), calls=%async_computation.9 | async-start | bytes 2621440 | tf_op jit(solution)/shard_map/all_gather | solution.py:170
  332.5 297.3 %reduce-scatter.21.cloned.1.call-start = ((), (), s32[]{:S(2)}) async-start(), calls=%async_computation.19 | async-start | bytes 884736
  345.8 285.9 %reduce-scatter.19.cloned.1.call-start = ((), (), s32[]{:S(2)}) async-start(), calls=%async_computation.18 | async-start | bytes 884736
  354.3 279.2 %all-reduce.10.cloned.1.call-start = ((), (), s32[]{:S(2)}) async-start(), calls=%async_computation.12 | async-start | bytes 2359296 | tf_op jit(solution)/shard_map/psum | solution.py:203
  531.5 114.3 %reduce-scatter.11.cloned.1.call-start = ((), (), s32[]{:S(2)}) async-start(), calls=%async_computation.6 | async-start | bytes 2949120 | tf_op jit(solution)/shard_map/reduce_scatter | solution.py:172
  536.8 144.3 %reduce-scatter.13.cloned.1.call-start = ((), (), s32[]{:S(2)}) async-start(), calls=%async_computation.7 | async-start | bytes 2949120 | tf_op jit(solution)/shard_map/reduce_scatter | solution.py:172
  543.4 173.1 %reduce-scatter.15.cloned.1.call-start = ((), (), s32[]{:S(2)}) async-start(), calls=%async_computation.8 | async-start | bytes 2949120 | tf_op jit(solution)/shard_map/reduce_scatter | solution.py:172
  548.4 204.0 %reduce-scatter.17.cloned.1.call-start = ((), (), s32[]{:S(2)}) async-start(), calls=%async_computation.10 | async-start | bytes 2949120 | tf_op jit(solution)/shard_map/reduce_scatter | solution.py:172
  (113 other events, 306.3 us)
Sparse Core Ops, SparseCore 0:
  318.1 211.1 all-reduce.7
  531.6 14.9 reduce-scatter.20
  549.4 15.3 reduce-scatter.18
  567.6 42.9 all-reduce.9
  612.9 32.8 reduce-scatter.10
  648.2 32.8 reduce-scatter.12
  683.6 32.8 reduce-scatter.14
  719.5 32.8 reduce-scatter.16
Sparse Core Ops, SparseCore 1:
  320.6 54.9 all-gather.13
  377.1 46.4 all-gather.15
  425.0 45.9 all-gather.17
  472.5 47.0 all-gather.19
  521.1 48.7 all-gather.21
  572.0 44.9 all-gather.11
where the time goes:
time: 768 us; the launch traced here: 760 us
  waiting for transfers between devices  365 us (48%)
  matrix products  184 us (24%)
  local copies, waits for them, and re-layouts  132 us (17%)
  other arithmetic  22.7 us (3%)
  blocking collectives  19.4 us (3%)
  starting transfers between devices  19.1 us (2%)
  between operations  17.6 us (2%)
    psum x1, waiting for transfers between devices, shards(): packed = lax.psum(packed, ('context', 'dp')).astype(jnp.float32)  175 us
    dot_general x78, matrix products, product(): return jnp.einsum(pattern, left, right, precision=highest)  120 us
    reduce_scatter x4, waiting for transfers between devices, weight_term(): lax.psum_scatter(term.astype(jnp.bfloat16), 'dp', scatter_dimension=0, ti...  113 us
    unnamed x192, local copies, waits for them, and re-layouts  65.9 us
    all_gather x4, waiting for transfers between devices, weight_term(): whole = lax.all_gather(columns, 'context', axis=0, tiled=True)  47.1 us
    all_gather x2, waiting for transfers between devices, slab_of(): whole = lax.all_gather(member, 'context', axis=0, tiled=True)  21.4 us
    dot_general x4, matrix products, weight_term(): jnp.einsum('tr,tc->rc', rows, whole, preferred_element_type=jnp.float32)  20.5 us
    ppermute x6, starting transfers between devices, shifted(): return lax.ppermute(value, axis, pairs)  18.2 us
  transfers between devices with their start and end apart: 20, of which 10 were waited for; matrix products, arithmetic and copies ran while one was open for 16% of the time, Pallas kernels for 0%

commit v1 on v0

--- a/solution.py
+++ b/solution.py
@@ -193,7 +193,8 @@
     down_term = jnp.einsum("td,tr->dr", gathered, low_grad, preferred_element_type=jnp.float32)
     small = [up_term, down_term, beta_term, bias_term]
     packed = jnp.concatenate([term.astype(jnp.bfloat16).reshape(-1, 128) for term in small], axis=0)
-    packed = lax.psum(packed, ("context", "dp")).astype(jnp.float32)
+    _write_group = lambda arr_in: jnp.sum(lax.all_gather(arr_in, axis_name=("context", "dp")), 0)
+    packed = _write_group(packed).astype(jnp.float32)
     results, start = ([], 0)
     for term in small:
         count = term.size // 128

time: 768 us -> 923 us (1.20)
  waiting for transfers between devices: 365 us -> 520 us
    psum x1 -> x0, waiting for transfers between devices: 175 us -> none  [shards(): packed = lax.psum(packed, ('context', 'dp')).astype(jnp.float32)]
    all_gather x0 -> x1, waiting for transfers between devices: none -> 95 us  [shards(): lax.all_gather(arr_in, axis_name=('context', 'dp'))]
    all_gather x4, waiting for transfers between devices: 47.1 us -> 137 us  [weight_term(): whole = lax.all_gather(columns, 'context', axis=0, tiled=True)]
    psum x1, waiting for transfers between devices: 0.01 us -> 45.7 us  [shards(): down_grad = lax.psum(down_grad, 'head')]
    ppermute x6, waiting for transfers between devices: 5.3 us -> 41.2 us  [shifted(): return lax.ppermute(value, axis, pairs)]
    all_gather x2, waiting for transfers between devices: 21.4 us -> 44.6 us  [slab_of(): whole = lax.all_gather(member, 'context', axis=0, tiled=True)]
    unnamed x16, waiting for transfers between devices: 2.58 us -> 24.4 us
    reduce_scatter x4, waiting for transfers between devices: 113 us -> 132 us  [weight_term(): lax.psum_scatter(term.astype(jnp.bfloat16), 'dp', scatter_dimension=0, ti...]
  transfers between devices with their start and end apart: 20 -> 20, of which waited for: 10 -> 17; matrix products, arithmetic and copies ran while one was open for 16% -> 24% of each run, Pallas kernels for 0% -> 0%
where the time goes in v1:
time: 923 us; the launch traced here: 915 us
  waiting for transfers between devices  520 us (56%)
  matrix products  182 us (20%)
  local copies, waits for them, and re-layouts  127 us (14%)
  other arithmetic  31.8 us (3%)
  starting transfers between devices  19.3 us (2%)
  blocking collectives  19.3 us (2%)
  between operations  16 us (2%)
    all_gather x4, waiting for transfers between devices, weight_term(): whole = lax.all_gather(columns, 'context', axis=0, tiled=True)  137 us
    reduce_scatter x4, waiting for transfers between devices, weight_term(): lax.psum_scatter(term.astype(jnp.bfloat16), 'dp', scatter_dimension=0, ti...  132 us
    dot_general x78, matrix products, product(): return jnp.einsum(pattern, left, right, precision=highest)  119 us
    all_gather x1, waiting for transfers between devices, shards(): lax.all_gather(arr_in, axis_name=('context', 'dp'))  95 us
    unnamed x196, local copies, waits for them, and re-layouts  61.7 us
    psum x1, waiting for transfers between devices, shards(): down_grad = lax.psum(down_grad, 'head')  45.7 us
    all_gather x2, waiting for transfers between devices, slab_of(): whole = lax.all_gather(member, 'context', axis=0, tiled=True)  44.6 us
    ppermute x6, waiting for transfers between devices, shifted(): return lax.ppermute(value, axis, pairs)  41.2 us
  transfers between devices with their start and end apart: 20, of which 17 were waited for; matrix products, arithmetic and copies ran while one was open for 24% of the time, Pallas kernels for 0%

profile of v1, /device:TPU:0, one launch (start us, length us, event | category | flops | bytes accessed | tf_op | source)
XLA Modules:
  0.0 915.4 jit_solution(2567976029094044964)
XLA Ops:
  7.3 11.0 %all_gather.30 = bf16[1,128,2304]{2,1,0:T(8,128)(2,1)S(1)} all-gather(bf16[1,128,1152]{2,1,0:T(8,128)(2,1)} %param.14), channel_id=1, replica_groups=mesh['context'=4,'dp'=4,'head'=2] {'head'}, dimensions={2}, use_global_device_ids=true | all-gather | bytes 884736 | tf_op jit(solution)/shard_map/all_gather | solution.py:117
  22.0 34.0 %copy.148 = bf16[2304,3,2048]{0,2,1:T(8,128)(2,1)} copy(bf16[2304,3,2048]{2,0,1:T(8,128)(2,1)} %param.16) | data formatting | bytes 56623104 | tf_op args[2]
  56.0 15.4 %fusion.134 = f32[128,3,16,128]{3,0,2,1:T(8,128)} fusion(bf16[3,16,128,2304]{3,2,1,0:T(8,128)(2,1)} %bitcast.474, bf16[1,128,2304]{2,1,0:T(8,128)(2,1)S(1)} %all_gather.30), kind=kOutput, calls=%fused_computation.216 | convolution fusion | flops 3623878656 | bytes 32047104 | tf_op jit(solution)/shard_map/dot_general | solution.py:123
  105.0 12.9 %while.51 = (s32[]{:T(128)}, f32[16,128,128]{2,1,0:T(8,128)}, f32[16,128,128]{2,1,0:T(8,128)}, f32[2,16,128,128]{3,2,1,0:T(8,128)}, f32[2,16,128,128]{3,2,1,0:T(8,128)}, /*index=5*/s32[]{:T(128)}, s32[]{:T(128)}) while((s32[]{:T(128)}, f32[16,128,128]{2,1,0:T(8,128)}, f32[16,128,128]{2,1,0:T(8,128)}, ...), condition=%wide.region_3.4_spmd.clone, body=%wide.region_2.0_spmd.clone.sunk | while | flops 403177472 | bytes 24118416 | solution.py:110
  132.9 8.3 all_gather.31
  141.2 13.1 %copy.250 = bf16[2048,2304]{1,0:T(8,128)(2,1)} copy(bf16[2048,2304]{0,1:T(8,128)(2,1)} %bitcast.484) | data formatting | bytes 18874368 | tf_op jit(solution)/shard_map/dot_general | solution.py:139
  192.2 30.7 %collective-permute-done.4 = bf16[16,128,128]{2,1,0:T(8,128)(2,1)S(1)} collective-permute-done((bf16[16,128,128]{2,1,0:T(8,128)(2,1)S(1)}, bf16[16,128,128]{2,1,0:T(8,128)(2,1)S(1)}, u32[]{:S(2)}, u32[]{:S(2)}) %collective-permute-start.4) | collective-permute-done | bytes 524320 | tf_op jit(solution)/shard_map/ppermute | solution.py:14
  227.4 9.6 %while.49 = (s32[]{:T(128)}, f32[16,128,128]{2,1,0:T(8,128)S(1)}, bf16[2,16,64,128]{3,2,0,1:T(8,128)(2,1)S(1)}, f32[2,16,128,128]{3,2,1,0:T(8,128)}, f32[2,16,12...) while((s32[]{:T(128)}, f32[16,128,128]{2,1,0:T(8,128)S(1)}, ...), condition=%wide.region_6.7_spmd, body=%wide.region_5.6_spmd.sunk | while | flops 302383104 | bytes 36178636 | solution.py:94
  237.1 7.2 collective-permute-done.5
  250.8 23.3 %while.50 = (s32[]{:T(128)}, f32[16,128,128]{2,1,0:T(8,128)S(1)}, f32[2,16,64,128]{3,2,0,1:T(8,128)}, f32[2,16,64,128]{3,2,1,0:T(8,128)}, f32[2,16,128,128]{2,3,...) while((s32[]{:T(128)}, f32[16,128,128]{2,1,0:T(8,128)S(1)}, ...), condition=%wide.region_9.10_spmd, body=%wide.region_8.9_spmd.sunk | while | flops 604241920 | bytes 56627016 | solution.py:94
  364.1 11.5 %fusion.57 = f32[128,2304]{1,0:T(8,128)S(1)} fusion(bf16[2304,6144]{0,1:T(8,128)(2,1)} %bitcast.475, bf16[128,2048]{0,1:T(8,128)(2,1)S(1)} %copy-done.93, bf16[128,2048]{0,1:T(8,128)(2,1)S(1)} %copy-done.92, bf16[128,2048]{0,1:T(8,128)(2,1)S(1)} %get-tuple-element.455), kind=kOutput, calls=%fused_computation.83 | convolution fusion | flops 3628597248 | bytes 31064064 | tf_op jit(solution)/shard_map/tc,dc->td/dot_general | solution.py:209
  385.3 8.6 all-gather.18.cloned.1.call-done
  399.3 40.6 %all-gather.20.cloned.1.call-done = bf16[512,1,2048]{0,2,1:T(8,128)(2,1)} async-done(((bf16[128,1,2048]{0,2,1:T(8,128)(2,1)}), bf16[512,1,2048]{0,2,1:T(8,128)(2,1)}) %all-gather.20.cloned.1.call-update) | async-done | bytes 2097168 | tf_op jit(solution)/shard_map/all_gather | solution.py:170
  444.8 41.0 %all-gather.22.cloned.1.call-done = bf16[512,1,2048]{0,2,1:T(8,128)(2,1)} async-done(((bf16[128,1,2048]{0,2,1:T(8,128)(2,1)}), bf16[512,1,2048]{0,2,1:T(8,128)(2,1)}) %all-gather.22.cloned.1.call-update) | async-done | bytes 2097168 | tf_op jit(solution)/shard_map/all_gather | solution.py:170
  490.8 44.6 %all-gather.24.cloned.1.call-done = bf16[1,512,2304]{2,1,0:T(8,128)(2,1)} async-done(((bf16[1,128,2304]{2,1,0:T(8,128)(2,1)}), bf16[1,512,2304]{2,1,0:T(8,128)(2,1)}) %all-gather.24.cloned.1.call-update) | async-done | bytes 2359312 | tf_op jit(solution)/shard_map/all_gather | solution.py:166
  535.4 47.0 %all-gather.14.cloned.1.call-done = bf16[512,2048]{0,1:T(8,128)(2,1)} async-done(((bf16[128,2048]{0,1:T(8,128)(2,1)}), bf16[512,2048]{0,1:T(8,128)(2,1)}) %all-gather.14.cloned.1.call-update) | async-done | bytes 2097168 | tf_op jit(solution)/shard_map/all_gather | solution.py:170
  587.7 95.0 %all-gather.26.cloned.1.call-done = bf16[74496,128]{1,0:T(8,128)(2,1)} async-done(((bf16[4656,128]{1,0:T(8,128)(2,1)}), bf16[74496,128]{1,0:T(8,128)(2,1)}) %all-gather.26.cloned.1.call-update) | async-done | bytes 19070992 | tf_op jit(solution)/shard_map/all_gather | solution.py:196
  682.7 10.5 %reduce_sum.155 = bf16[4656,128]{1,0:T(8,128)(2,1)S(1)} reduce(bf16[16,4656,128]{2,1,0:T(8,128)(2,1)} %bitcast.490, bf16[]{:T(256)} %constant.94.clone.1), dimensions={0}, to_apply=%region_26.27 | reduce | flops 8939520 | bytes 20262914 | tf_op jit(solution)/shard_map/reduce_sum | solution.py:196
  702.1 16.4 %reduce-scatter.19.cloned.1.call-done = bf16[1152,128]{1,0:T(8,128)(2,1)} async-done(((bf16[2304,128]{1,0:T(8,128)(2,1)}), bf16[1152,128]{1,0:T(8,128)(2,1)}) %reduce-scatter.19.cloned.1.call-update) | async-done | bytes 294928
  720.4 33.4 %reduce-scatter.11.cloned.1.call-done = bf16[144,2048]{1,0:T(8,128)(2,1)} async-done(((bf16[576,2048]{1,0:T(8,128)(2,1)}), bf16[144,2048]{1,0:T(8,128)(2,1)}) %reduce-scatter.11.cloned.1.call-update) | async-done | bytes 589840 | tf_op jit(solution)/shard_map/reduce_scatter | solution.py:172
  753.7 35.4 %reduce-scatter.13.cloned.1.call-done = bf16[144,2048]{1,0:T(8,128)(2,1)} async-done(((bf16[576,2048]{1,0:T(8,128)(2,1)}), bf16[144,2048]{1,0:T(8,128)(2,1)}) %reduce-scatter.13.cloned.1.call-update) | async-done | bytes 589840 | tf_op jit(solution)/shard_map/reduce_scatter | solution.py:172
  789.1 35.2 %reduce-scatter.15.cloned.1.call-done = bf16[144,2048]{1,0:T(8,128)(2,1)} async-done(((bf16[576,2048]{1,0:T(8,128)(2,1)}), bf16[144,2048]{1,0:T(8,128)(2,1)}) %reduce-scatter.15.cloned.1.call-update) | async-done | bytes 589840 | tf_op jit(solution)/shard_map/reduce_scatter | solution.py:172
  832.6 27.7 %reduce-scatter.17.cloned.1.call-done = bf16[144,2048]{1,0:T(8,128)(2,1)} async-done(((bf16[576,2048]{1,0:T(8,128)(2,1)}), bf16[144,2048]{1,0:T(8,128)(2,1)}) %reduce-scatter.17.cloned.1.call-update) | async-done | bytes 589840 | tf_op jit(solution)/shard_map/reduce_scatter | solution.py:172
  860.3 45.7 %all-reduce.7.cloned.1.call-done = f32[2304,128]{1,0:T(8,128)} async-done(((f32[2304,128]{1,0:T(8,128)}), f32[2304,128]{1,0:T(8,128)}) %all-reduce.7.cloned.1.call-update) | async-done | bytes 1179664 | tf_op jit(solution)/shard_map/psum | solution.py:204
  (456 shorter events, 286.8 us)
Async XLA Ops:
  7.2 378.1 %all-gather.16.cloned.1.call-start = ((), (), s32[]{:S(2)}) async-start(), calls=%async_computation.12 | async-start | bytes 2949120 | tf_op jit(solution)/shard_map/all_gather | solution.py:166
  18.3 57.6 %copy-start.36 = (bf16[1,128,2304]{2,1,0:T(8,128)(2,1)}, bf16[1,128,2304]{2,1,0:T(8,128)(2,1)S(1)}, u32[]{:S(2)}) copy-start(bf16[1,128,2304]{2,1,0:T(8,128)(2,1)S(1)} %all_gather.30) | copy-start | bytes 1769476
  79.1 45.5 %copy-start.3 = (f32[128,16,128]{2,0,1:T(8,128)}, f32[128,16,128]{2,0,1:T(8,128)S(1)}, u32[]{:S(2)}) copy-start(f32[128,16,128]{2,0,1:T(8,128)S(1)} %get-tuple-element.451) | copy-start | bytes 3145732
  120.2 47.6 %collective-permute-start = (bf16[16,128,128]{2,1,0:T(8,128)(2,1)}, bf16[16,128,128]{2,1,0:T(8,128)(2,1)}, u32[]{:S(2)}, u32[]{:S(2)}) collective-permute-start(bf16[16,128,128]{2,1,0:T(8,128)(2,1)} %convert_element_type.155), channel_id=1, source_target_pairs={{0,8},{8,16},{16,24},{1,9},{9,17},{17,25},{2,10},{10,18},{18,26},{... | collective-permute-start | bytes 1572872 | tf_op jit(solution)/shard_map/ppermute | solution.py:14
  128.2 31.8 %copy-start.72 = (f32[16,2,64,128]{3,2,1,0:T(8,128)}, f32[16,2,64,128]{3,2,1,0:T(8,128)S(1)}, u32[]{:S(2)}) copy-start(f32[16,2,64,128]{3,2,1,0:T(8,128)S(1)} %convolution_subtract_fusion) | copy-start | bytes 3145732
  166.5 13.9 %collective-permute-start.3 = (bf16[16,128,128]{2,1,0:T(8,128)(2,1)}, bf16[16,128,128]{2,1,0:T(8,128)(2,1)}, u32[]{:S(2)}, u32[]{:S(2)}) collective-permute-start(bf16[16,128,128]{2,1,0:T(8,128)(2,1)} %get-tuple-element.466), channel_id=1, source_target_pairs={{8,0},{16,8},{24,16},{9,1},{17,9},{25,17},{10,2},{18,10},{26,18},{... | collective-permute-start | bytes 1572872 | tf_op jit(solution)/shard_map/ppermute | solution.py:14
  170.1 14.4 %collective-permute-start.1 = (bf16[16,128,128]{2,1,0:T(8,128)(2,1)}, bf16[16,128,128]{2,1,0:T(8,128)(2,1)}, u32[]{:S(2)}, u32[]{:S(2)}) collective-permute-start(bf16[16,128,128]{2,1,0:T(8,128)(2,1)} %fusion.77), channel_id=1, source_target_pairs={{0,8},{8,16},{16,24},{1,9},{9,17},{17,25},{2,10},{10,18},{18,26},{... | collective-permute-start | bytes 1572872 | tf_op jit(solution)/shard_map/ppermute | solution.py:14
  175.5 218.3 %all-gather.18.cloned.1.call-start = ((), (), s32[]{:S(2)}) async-start(), calls=%async_computation.13 | async-start | bytes 2621440 | tf_op jit(solution)/shard_map/all_gather | solution.py:170
  182.2 40.8 %collective-permute-start.4 = (bf16[16,128,128]{2,1,0:T(8,128)(2,1)S(1)}, bf16[16,128,128]{2,1,0:T(8,128)(2,1)S(1)}, u32[]{:S(2)}, u32[]{:S(2)}) collective-permute-start(bf16[16,128,128]{2,1,0:T(8,128)(2,1)S(1)} %fusion.79), channel_id=1, source_target_pairs={{8,0},{16,8},{24,16},{9,1},{17,9},{25,17},{10,2},{18,10},{26,18},{... | collective-permute-start | bytes 1572872 | tf_op jit(solution)/shard_map/ppermute | solution.py:14
  186.1 39.6 %collective-permute-start.2 = (bf16[16,128,128]{2,1,0:T(8,128)(2,1)S(1)}, bf16[16,128,128]{2,1,0:T(8,128)(2,1)S(1)}, u32[]{:S(2)}, u32[]{:S(2)}) collective-permute-start(bf16[16,128,128]{2,1,0:T(8,128)(2,1)S(1)} %fusion.78), channel_id=1, source_target_pairs={{0,8},{8,16},{16,24},{1,9},{9,17},{17,25},{2,10},{10,18},{18,26},{... | collective-permute-start | bytes 1572872 | tf_op jit(solution)/shard_map/ppermute | solution.py:14
  224.5 19.8 %collective-permute-start.5 = (bf16[16,128,128]{2,1,0:T(8,128)(2,1)}, bf16[16,128,128]{2,1,0:T(8,128)(2,1)}, u32[]{:S(2)}, u32[]{:S(2)}) collective-permute-start(bf16[16,128,128]{2,1,0:T(8,128)(2,1)} %fusion.80), channel_id=1, source_target_pairs={{8,0},{16,8},{24,16},{9,1},{17,9},{25,17},{10,2},{18,10},{26,18},{... | collective-permute-start | bytes 1572872 | tf_op jit(solution)/shard_map/ppermute | solution.py:14
  349.0 90.9 %all-gather.20.cloned.1.call-start = ((), (), s32[]{:S(2)}) async-start(), calls=%async_computation.14 | async-start | bytes 2621440 | tf_op jit(solution)/shard_map/all_gather | solution.py:170
  349.8 136.0 %all-gather.22.cloned.1.call-start = ((), (), s32[]{:S(2)}) async-start(), calls=%async_computation.15 | async-start | bytes 2621440 | tf_op jit(solution)/shard_map/all_gather | solution.py:170
  350.4 185.1 %all-gather.24.cloned.1.call-start = ((), (), s32[]{:S(2)}) async-start(), calls=%async_computation.16 | async-start | bytes 2949120 | tf_op jit(solution)/shard_map/all_gather | solution.py:166
  350.9 231.5 %all-gather.14.cloned.1.call-start = ((), (), s32[]{:S(2)}) async-start(), calls=%async_computation.9 | async-start | bytes 2621440 | tf_op jit(solution)/shard_map/all_gather | solution.py:170
  352.2 330.4 %all-gather.26.cloned.1.call-start = ((), (), s32[]{:S(2)}) async-start(), calls=%async_computation.17 | async-start | bytes 20262912 | tf_op jit(solution)/shard_map/all_gather | solution.py:196
  362.9 337.4 %reduce-scatter.21.cloned.1.call-start = ((), (), s32[]{:S(2)}) async-start(), calls=%async_computation.19 | async-start | bytes 884736
  377.1 341.5 %reduce-scatter.19.cloned.1.call-start = ((), (), s32[]{:S(2)}) async-start(), calls=%async_computation.18 | async-start | bytes 884736
  385.2 368.5 %reduce-scatter.11.cloned.1.call-start = ((), (), s32[]{:S(2)}) async-start(), calls=%async_computation.6 | async-start | bytes 2949120 | tf_op jit(solution)/shard_map/reduce_scatter | solution.py:172
  399.0 40.9 %copy-start.104 = (bf16[1,512,2304]{2,1,0:T(8,128)(2,1)S(1)}, bf16[1,512,2304]{2,1,0:T(8,128)(2,1)}, u32[]{:S(2)}) copy-start(bf16[1,512,2304]{2,1,0:T(8,128)(2,1)} %all-gather.16.cloned.1.call-done) | copy-start | bytes 7077892
  399.0 390.1 %reduce-scatter.13.cloned.1.call-start = ((), (), s32[]{:S(2)}) async-start(), calls=%async_computation.7 | async-start | bytes 2949120 | tf_op jit(solution)/shard_map/reduce_scatter | solution.py:172
  444.8 379.6 %reduce-scatter.15.cloned.1.call-start = ((), (), s32[]{:S(2)}) async-start(), calls=%async_computation.8 | async-start | bytes 2949120 | tf_op jit(solution)/shard_map/reduce_scatter | solution.py:172
  490.8 369.5 %reduce-scatter.17.cloned.1.call-start = ((), (), s32[]{:S(2)}) async-start(), calls=%async_computation.10 | async-start | bytes 2949120 | tf_op jit(solution)/shard_map/reduce_scatter | solution.py:172
  587.6 318.4 %all-reduce.7.cloned.1.call-start = ((), (), s32[]{:S(2)}) async-start(), calls=%async_computation.11 | async-start | bytes 2359296 | tf_op jit(solution)/shard_map/psum | solution.py:204
  (115 other events, 342.7 us)
Sparse Core Ops, SparseCore 0:
  175.6 63.9 all-gather.15
  349.2 44.6 all-gather.17
  395.4 44.4 all-gather.19
  441.3 44.4 all-gather.21
  487.2 48.1 all-gather.23
  537.4 45.0 all-gather.13
  584.6 97.9 all-gather.25
  684.9 15.3 reduce-scatter.20
  703.1 15.3 reduce-scatter.18
  720.9 32.7 reduce-scatter.10
  756.3 32.8 reduce-scatter.12
  791.5 32.8 reduce-scatter.14
  827.5 32.8 reduce-scatter.16
  863.0 42.9 all-reduce.6
